TPU v7x, 32 devices: a whole 2x2x4 slice. The times are simulated.
32 devices in a mesh: seq: 8 (over y, x, core), tensor: 4 (over z).
Axes of the slice: x: 2, y: 2, z: 4, core: 2. Of those that a mesh axis runs over, the one named last changes fastest.
Arguments:
- patches: bfloat16 [2048, 6144], P('seq', 'tensor'), may hold values from -60 to 60
- segment_ids: int32 [2048], replicated, may hold values from 0 to 3, never falling along the last dimension, each value on 1 to 768 neighbouring positions
- w_query: bfloat16 [6144, 1024], P('seq', 'tensor'), may hold values from -0.078125 to 0.078125
- w_key: bfloat16 [6144, 1024], P('seq', 'tensor'), may hold values from -0.078125 to 0.078125
- w_value: bfloat16 [6144, 1024], P('seq', 'tensor'), may hold values from -0.078125 to 0.078125
- w_out: bfloat16 [1024, 6144], P('seq', 'tensor'), may hold values from -0.1875 to 0.1875
Outputs:
- attended: bfloat16 [2048, 6144], P('seq', 'tensor')
Inputs may be any that keep to these rules, and one draw needn't show every extreme that they name: `segment_ids`: image ids never fall along the row; every image holds at most 768 patches and some image exactly that many.
All inputs are finite; a program needn't handle non-finite values.
Results may differ from a plain program's by a relative error of at most 0.012.
The roundings to bfloat16 on the way count: a program that leaves them out, or rounds other values in their place, can miss the bound.
Values may be sent and summed in bfloat16 or wider, within the bound.
No kernel may reach another device: no remote copies, remote signals or barrier semaphores. Data moves between devices by JAX's collectives and lax.ppermute only.
A program may use at most 64 MiB of HBM per device.

v0:
```python
import jax
import jax.numpy as jnp
from jax import lax
from jax.sharding import PartitionSpec as P

HS = 128
SPAN = 3


def shifted(x, axis, by):
    count = lax.axis_size(axis)
    pairs = [(i, i + by) for i in range(count) if 0 <= i + by < count]
    return lax.ppermute(x, axis, pairs)


def on_device(patches, segment_ids, w_query, w_key, w_value, w_out):
    tok_rows = patches.shape[0]
    col_width = w_query.shape[1]
    local_heads = col_width // HS
    seq_count = lax.axis_size("seq")
    device = lax.axis_index("seq")
    gathered = lax.all_gather(patches, "tensor", axis=1, tiled=True)
    pieces = (
        lax.all_gather(w_query, "seq", axis=0, tiled=True),
        lax.all_gather(w_key, "seq", axis=0, tiled=True),
        lax.all_gather(w_value, "seq", axis=0, tiled=True),
    )
    sums = tuple((jnp.dot(gathered, piece, preferred_element_type=jnp.float32) for piece in pieces))
    queries, keys_here, values_here = [
        item.astype(jnp.bfloat16).reshape(tok_rows, local_heads, HS) for item in sums
    ]

    def source_ids(offset_by):
        source = device - offset_by
        inside = (source >= 0) & (source < seq_count)
        begin = jnp.clip(source, 0, seq_count - 1) * tok_rows
        picked = lax.dynamic_slice_in_dim(segment_ids, begin, tok_rows)
        return jnp.where(inside, picked, -1)

    blocks = [(0, keys_here, values_here)]
    offsets = list(range(1, SPAN + 1)) + [-depth for depth in range(1, SPAN + 1)]
    for offset_by in offsets:
        moved = shifted((keys_here, values_here), "seq", offset_by)
        blocks.append((offset_by, moved[0], moved[1]))
    key_block = jnp.concatenate([entry[1] for entry in blocks], 0)
    value_block = jnp.concatenate([entry[2] for entry in blocks], 0)
    key_ids = jnp.concatenate([source_ids(entry[0]) for entry in blocks], 0)
    own_ids = source_ids(0)
    scaling = HS ** (-0.5)
    scores = (
        jnp.einsum("qhd,khd->hqk", queries, key_block, preferred_element_type=jnp.float32) * scaling
    )
    same_image = (own_ids[:, None] == key_ids[None, :])[None]
    scores = jnp.where(same_image, scores, -jnp.inf)
    weights_bf = jax.nn.softmax(scores, axis=-1).astype(jnp.bfloat16)
    heads_out = jnp.einsum(
        "hqk,khd->qhd", weights_bf, value_block, preferred_element_type=jnp.float32
    )
    heads_out = heads_out.astype(jnp.bfloat16).reshape(tok_rows, col_width)
    out_full = lax.all_gather(w_out, "seq", axis=0, tiled=True)
    attended = jnp.dot(
        lax.all_gather(heads_out, "tensor", axis=1, tiled=True),
        out_full,
        preferred_element_type=jnp.float32,
    )
    return attended.astype(jnp.bfloat16)


def solution(mesh):
    in_specs = (
        P("seq", "tensor"),
        P(),
        P("seq", "tensor"),
        P("seq", "tensor"),
        P("seq", "tensor"),
        P("seq", "tensor"),
    )
    out_specs = P("seq", "tensor")
    return jax.shard_map(
        on_device, mesh=mesh, in_specs=in_specs, out_specs=out_specs, check_vma=False
    )
```

profile of v0, /device:TPU:0, one launch (start us, length us, event | category | flops | bytes accessed | tf_op | source)
XLA Modules:
  0.0 243.4 jit_solution(93550354333636955)
XLA Ops:
  10.0 0.8 constant_dynamic-update-slice_fusion.7
  13.8 0.8 constant_dynamic-update-slice_fusion.16
  15.4 1.1 broadcast_compare_fusion
  16.4 58.7 %all-gather.6.cloned.1.call-done = bf16[256,6144]{1,0:T(8,128)(2,1)} async-done(((bf16[256,1536]{1,0:T(8,128)(2,1)}), bf16[256,6144]{1,0:T(8,128)(2,1)}) %all-gather.6.cloned.1.call-update) | async-done | bytes 3145744 | tf_op jit(solution)/shard_map/all_gather | solution.py:22
  75.1 32.7 %all-gather.8.cloned.1.call-done = bf16[6144,256]{1,0:T(8,128)(2,1)} async-done(((bf16[768,256]{1,0:T(8,128)(2,1)}), bf16[6144,256]{1,0:T(8,128)(2,1)}) %all-gather.8.cloned.1.call-update) | async-done | bytes 3145744 | tf_op jit(solution)/shard_map/all_gather | solution.py:26
  107.8 4.2 %convolution_convert_fusion.3 = bf16[256,256]{0,1:T(8,128)(2,1)S(1)} fusion(bf16[256,6144]{1,0:T(8,128)(2,1)} %all-gather.6.cloned.1.call-done, bf16[6144,256]{1,0:T(8,128)(2,1)} %all-gather.8.cloned.1.call-done), kind=kOutput, calls=%fused_computation.10 | convolution fusion | flops 805371904 | bytes 6422528 | tf_op jit(solution)/shard_map/dot_general | solution.py:28
  112.0 1.3 collective-permute-start.5
  113.3 1.3 collective-permute-start.4
  114.6 1.3 collective-permute-start.3
  115.9 5.8 %collective-permute-start.1 = (bf16[256,2,128]{0,2,1:T(8,128)(2,1)S(1)}, bf16[256,2,128]{0,2,1:T(8,128)(2,1)}, u32[]{:S(2)}, u32[]{:S(2)}) collective-permute-start(bf16[256,2,128]{0,2,1:T(8,128)(2,1)S(1)} %bitcast.22), channel_id=1, source_target_pairs={{0,8},{4,12},{8,16},{12,20},{16,24},{20,28},{1,9},{5,13},{9,17},{1... | collective-permute-start | bytes 393224 | tf_op jit(solution)/shard_map/ppermute | solution.py:13
  121.8 3.0 %collective-permute-start = (bf16[256,2,128]{0,2,1:T(8,128)(2,1)S(1)}, bf16[256,2,128]{0,2,1:T(8,128)(2,1)}, u32[]{:S(2)}, u32[]{:S(2)}) collective-permute-start(bf16[256,2,128]{0,2,1:T(8,128)(2,1)S(1)} %bitcast.23), channel_id=1, source_target_pairs={{0,4},{4,8},{8,12},{12,16},{16,20},{20,24},{24,28},{1,5},{5,9},{9,... | collective-permute-start | bytes 393224 | tf_op jit(solution)/shard_map/ppermute | solution.py:13
  124.8 21.1 %all-gather.10.cloned.1.call-done = bf16[6144,256]{1,0:T(8,128)(2,1)} async-done(((bf16[768,256]{1,0:T(8,128)(2,1)}), bf16[6144,256]{1,0:T(8,128)(2,1)}) %all-gather.10.cloned.1.call-update) | async-done | bytes 3145744 | tf_op jit(solution)/shard_map/all_gather | solution.py:24
  145.9 3.2 %convolution_convert_fusion.2 = bf16[256,256]{0,1:T(8,128)(2,1)S(1)} fusion(bf16[256,6144]{1,0:T(8,128)(2,1)S(1)} %copy-done, bf16[6144,256]{1,0:T(8,128)(2,1)} %all-gather.10.cloned.1.call-done), kind=kOutput, calls=%fused_computation.9 | convolution fusion | flops 805371904 | bytes 6422528 | tf_op jit(solution)/shard_map/dot_general | solution.py:28
  149.1 30.7 %all-gather.12.cloned.1.call-done = bf16[6144,256]{1,0:T(8,128)(2,1)} async-done(((bf16[768,256]{1,0:T(8,128)(2,1)}), bf16[6144,256]{1,0:T(8,128)(2,1)}) %all-gather.12.cloned.1.call-update) | async-done | bytes 3145744 | tf_op jit(solution)/shard_map/all_gather | solution.py:25
  179.9 3.2 %convolution_convert_fusion.1 = bf16[256,256]{0,1:T(8,128)(2,1)S(1)} fusion(bf16[256,6144]{1,0:T(8,128)(2,1)S(1)} %copy-done, bf16[6144,256]{1,0:T(8,128)(2,1)} %all-gather.12.cloned.1.call-done), kind=kOutput, calls=%fused_computation.8 | convolution fusion | flops 805371904 | bytes 6422528 | tf_op jit(solution)/shard_map/dot_general | solution.py:28
  183.3 3.2 %collective-permute-start.2 = (bf16[256,2,128]{0,2,1:T(8,128)(2,1)S(1)}, bf16[256,2,128]{0,2,1:T(8,128)(2,1)S(1)}, u32[]{:S(2)}, u32[]{:S(2)}) collective-permute-start(bf16[256,2,128]{0,2,1:T(8,128)(2,1)S(1)} %bitcast.25), channel_id=1, source_target_pairs={{0,12},{4,16},{8,20},{12,24},{16,28},{1,13},{5,17},{9,21},{13,25},... | collective-permute-start | bytes 393224 | tf_op jit(solution)/shard_map/ppermute | solution.py:13
  186.5 0.9 constant_dynamic-update-slice_fusion.5
  187.4 1.3 collective-permute-start.11
  188.7 0.9 constant_dynamic-update-slice_fusion.4
  189.7 1.3 collective-permute-start.10
  191.0 1.3 collective-permute-start.9
  192.3 0.9 constant_dynamic-update-slice_fusion.2
  193.2 3.0 %collective-permute-start.6 = (bf16[256,2,128]{2,0,1:T(8,128)(2,1)S(1)}, bf16[256,2,128]{2,0,1:T(8,128)(2,1)S(1)}, u32[]{:S(2)}, u32[]{:S(2)}) collective-permute-start(bf16[256,2,128]{2,0,1:T(8,128)(2,1)S(1)} %copy.13), channel_id=1, source_target_pairs={{0,4},{4,8},{8,12},{12,16},{16,20},{20,24},{24,28},{1,5},{5,9},{9,... | collective-permute-start | bytes 393224 | tf_op jit(solution)/shard_map/ppermute | solution.py:13
  196.3 0.9 constant_dynamic-update-slice_fusion.1
  197.2 4.8 %collective-permute-start.7 = (bf16[256,2,128]{2,0,1:T(8,128)(2,1)S(1)}, bf16[256,2,128]{2,0,1:T(8,128)(2,1)S(1)}, u32[]{:S(2)}, u32[]{:S(2)}) collective-permute-start(bf16[256,2,128]{2,0,1:T(8,128)(2,1)S(1)} %copy.13), channel_id=1, source_target_pairs={{0,8},{4,12},{8,16},{12,20},{16,24},{20,28},{1,9},{5,13},{9,17},{1... | collective-permute-start | bytes 393224 | tf_op jit(solution)/shard_map/ppermute | solution.py:13
  202.0 0.9 constant_dynamic-update-slice_fusion
  202.9 5.6 %collective-permute-start.8 = (bf16[256,2,128]{2,0,1:T(8,128)(2,1)S(1)}, bf16[256,2,128]{2,0,1:T(8,128)(2,1)S(1)}, u32[]{:S(2)}, u32[]{:S(2)}) collective-permute-start(bf16[256,2,128]{2,0,1:T(8,128)(2,1)S(1)} %copy.13), channel_id=1, source_target_pairs={{0,12},{4,16},{8,20},{12,24},{16,28},{1,13},{5,17},{9,21},{13,25},... | collective-permute-start | bytes 393224 | tf_op jit(solution)/shard_map/ppermute | solution.py:13
  208.6 5.1 %collective-permute-done.8 = bf16[256,2,128]{2,0,1:T(8,128)(2,1)S(1)} collective-permute-done((bf16[256,2,128]{2,0,1:T(8,128)(2,1)S(1)}, bf16[256,2,128]{2,0,1:T(8,128)(2,1)S(1)}, u32[]{:S(2)}, u32[]{:S(2)}) %collective-permute-start.8) | collective-permute-done | bytes 131104 | tf_op jit(solution)/shard_map/ppermute | solution.py:13
  213.9 1.5 exponential_reduce_fusion
  215.4 1.9 fusion.3
  217.3 15.7 %all_gather.22 = bf16[256,1024]{0,1:T(8,128)(2,1)S(1)} all-gather(bf16[256,256]{0,1:T(8,128)(2,1)S(1)} %bitcast.29), channel_id=1, replica_groups=mesh['seq'=8,'tensor'=4] {'tensor'}, dimensions={1}, use_global_device_ids=true | all-gather | bytes 655360 | tf_op jit(solution)/shard_map/all_gather | solution.py:62
  233.1 3.8 %convolution_convert_fusion = bf16[256,1536]{1,0:T(8,128)(2,1)} fusion(bf16[256,1024]{0,1:T(8,128)(2,1)S(1)} %all_gather.22, bf16[1024,1536]{1,0:T(8,128)(2,1)} %all-gather.14.cloned.1.call-done), kind=kOutput, calls=%fused_computation.5 | convolution fusion | flops 805699584 | bytes 4456448 | tf_op jit(solution)/shard_map/dot_general | solution.py:61
  (42 shorter events, 7.4 us)
Async XLA Ops:
  6.5 68.6 %all-gather.6.cloned.1.call-start = ((), (), s32[]{:S(2)}) async-start(), calls=%async_computation | async-start | bytes 3932160 | tf_op jit(solution)/shard_map/all_gather | solution.py:22
  7.3 100.6 %all-gather.8.cloned.1.call-start = ((), (), s32[]{:S(2)}) async-start(), calls=%async_computation.1 | async-start | bytes 3538944 | tf_op jit(solution)/shard_map/all_gather | solution.py:26
  8.0 137.9 %all-gather.10.cloned.1.call-start = ((), (), s32[]{:S(2)}) async-start(), calls=%async_computation.2 | async-start | bytes 3538944 | tf_op jit(solution)/shard_map/all_gather | solution.py:24
  8.7 171.1 %all-gather.12.cloned.1.call-start = ((), (), s32[]{:S(2)}) async-start(), calls=%async_computation.3 | async-start | bytes 3538944 | tf_op jit(solution)/shard_map/all_gather | solution.py:25
  9.3 223.8 %all-gather.14.cloned.1.call-start = ((), (), s32[]{:S(2)}) async-start(), calls=%async_computation.4 | async-start | bytes 3538944 | tf_op jit(solution)/shard_map/all_gather | solution.py:60
  75.1 70.8 %copy-start = (bf16[256,6144]{1,0:T(8,128)(2,1)S(1)}, bf16[256,6144]{1,0:T(8,128)(2,1)}, u32[]{:S(2)}) copy-start(bf16[256,6144]{1,0:T(8,128)(2,1)} %all-gather.6.cloned.1.call-done) | copy-start | bytes 9437188
  112.0 85.2 %collective-permute-start.5 = (bf16[256,2,128]{0,2,1:T(8,128)(2,1)S(1)}, bf16[256,2,128]{0,2,1:T(8,128)(2,1)}, u32[]{:S(2)}, u32[]{:S(2)}) collective-permute-start(bf16[256,2,128]{0,2,1:T(8,128)(2,1)S(1)} %bitcast.19), channel_id=1, source_target_pairs={{12,0},{16,4},{20,8},{24,12},{28,16},{13,1},{17,5},{21,9},{25,13},... | collective-permute-start | bytes 393224 | tf_op jit(solution)/shard_map/ppermute | solution.py:13
  113.3 79.9 %collective-permute-start.4 = (bf16[256,2,128]{0,2,1:T(8,128)(2,1)S(1)}, bf16[256,2,128]{0,2,1:T(8,128)(2,1)}, u32[]{:S(2)}, u32[]{:S(2)}) collective-permute-start(bf16[256,2,128]{0,2,1:T(8,128)(2,1)S(1)} %bitcast.20), channel_id=1, source_target_pairs={{8,0},{12,4},{16,8},{20,12},{24,16},{28,20},{9,1},{13,5},{17,9},{2... | collective-permute-start | bytes 393224 | tf_op jit(solution)/shard_map/ppermute | solution.py:13
  114.6 76.4 %collective-permute-start.3 = (bf16[256,2,128]{0,2,1:T(8,128)(2,1)S(1)}, bf16[256,2,128]{0,2,1:T(8,128)(2,1)}, u32[]{:S(2)}, u32[]{:S(2)}) collective-permute-start(bf16[256,2,128]{0,2,1:T(8,128)(2,1)S(1)} %bitcast.21), channel_id=1, source_target_pairs={{4,0},{8,4},{12,8},{16,12},{20,16},{24,20},{28,24},{5,1},{9,5},{13... | collective-permute-start | bytes 393224 | tf_op jit(solution)/shard_map/ppermute | solution.py:13
  115.9 71.5 %collective-permute-start.1 = (bf16[256,2,128]{0,2,1:T(8,128)(2,1)S(1)}, bf16[256,2,128]{0,2,1:T(8,128)(2,1)}, u32[]{:S(2)}, u32[]{:S(2)}) collective-permute-start(bf16[256,2,128]{0,2,1:T(8,128)(2,1)S(1)} %bitcast.22), channel_id=1, source_target_pairs={{0,8},{4,12},{8,16},{12,20},{16,24},{20,28},{1,9},{5,13},{9,17},{1... | collective-permute-start | bytes 393224 | tf_op jit(solution)/shard_map/ppermute | solution.py:13
  121.8 61.5 %collective-permute-start = (bf16[256,2,128]{0,2,1:T(8,128)(2,1)S(1)}, bf16[256,2,128]{0,2,1:T(8,128)(2,1)}, u32[]{:S(2)}, u32[]{:S(2)}) collective-permute-start(bf16[256,2,128]{0,2,1:T(8,128)(2,1)S(1)} %bitcast.23), channel_id=1, source_target_pairs={{0,4},{4,8},{8,12},{12,16},{16,20},{20,24},{24,28},{1,5},{5,9},{9,... | collective-permute-start | bytes 393224 | tf_op jit(solution)/shard_map/ppermute | solution.py:13
  183.1 30.8 %copy-start.1 = (pred[256,1792]{1,0:T(8,128)(4,1)S(1)}, pred[256,1792]{1,0:T(8,128)(4,1)}, u32[]{:S(2)}) copy-start(pred[256,1792]{1,0:T(8,128)(4,1)} %broadcast_compare_fusion) | copy-start | bytes 1376260
  183.3 6.4 %collective-permute-start.2 = (bf16[256,2,128]{0,2,1:T(8,128)(2,1)S(1)}, bf16[256,2,128]{0,2,1:T(8,128)(2,1)S(1)}, u32[]{:S(2)}, u32[]{:S(2)}) collective-permute-start(bf16[256,2,128]{0,2,1:T(8,128)(2,1)S(1)} %bitcast.25), channel_id=1, source_target_pairs={{0,12},{4,16},{8,20},{12,24},{16,28},{1,13},{5,17},{9,21},{13,25},... | collective-permute-start | bytes 393224 | tf_op jit(solution)/shard_map/ppermute | solution.py:13
  187.4 26.4 %collective-permute-start.11 = (bf16[256,2,128]{2,0,1:T(8,128)(2,1)S(1)}, bf16[256,2,128]{2,0,1:T(8,128)(2,1)S(1)}, u32[]{:S(2)}, u32[]{:S(2)}) collective-permute-start(bf16[256,2,128]{2,0,1:T(8,128)(2,1)S(1)} %copy.13), channel_id=1, source_target_pairs={{12,0},{16,4},{20,8},{24,12},{28,16},{13,1},{17,5},{21,9},{25,13},... | collective-permute-start | bytes 393224 | tf_op jit(solution)/shard_map/ppermute | solution.py:13
  189.7 24.1 %collective-permute-start.10 = (bf16[256,2,128]{2,0,1:T(8,128)(2,1)S(1)}, bf16[256,2,128]{2,0,1:T(8,128)(2,1)S(1)}, u32[]{:S(2)}, u32[]{:S(2)}) collective-permute-start(bf16[256,2,128]{2,0,1:T(8,128)(2,1)S(1)} %copy.13), channel_id=1, source_target_pairs={{8,0},{12,4},{16,8},{20,12},{24,16},{28,20},{9,1},{13,5},{17,9},{2... | collective-permute-start | bytes 393224 | tf_op jit(solution)/shard_map/ppermute | solution.py:13
  191.0 22.8 %collective-permute-start.9 = (bf16[256,2,128]{2,0,1:T(8,128)(2,1)S(1)}, bf16[256,2,128]{2,0,1:T(8,128)(2,1)S(1)}, u32[]{:S(2)}, u32[]{:S(2)}) collective-permute-start(bf16[256,2,128]{2,0,1:T(8,128)(2,1)S(1)} %copy.13), channel_id=1, source_target_pairs={{4,0},{8,4},{12,8},{16,12},{20,16},{24,20},{28,24},{5,1},{9,5},{13... | collective-permute-start | bytes 393224 | tf_op jit(solution)/shard_map/ppermute | solution.py:13
  193.2 9.7 %collective-permute-start.6 = (bf16[256,2,128]{2,0,1:T(8,128)(2,1)S(1)}, bf16[256,2,128]{2,0,1:T(8,128)(2,1)S(1)}, u32[]{:S(2)}, u32[]{:S(2)}) collective-permute-start(bf16[256,2,128]{2,0,1:T(8,128)(2,1)S(1)} %copy.13), channel_id=1, source_target_pairs={{0,4},{4,8},{8,12},{12,16},{16,20},{20,24},{24,28},{1,5},{5,9},{9,... | collective-permute-start | bytes 393224 | tf_op jit(solution)/shard_map/ppermute | solution.py:13
  197.2 11.4 %collective-permute-start.7 = (bf16[256,2,128]{2,0,1:T(8,128)(2,1)S(1)}, bf16[256,2,128]{2,0,1:T(8,128)(2,1)S(1)}, u32[]{:S(2)}, u32[]{:S(2)}) collective-permute-start(bf16[256,2,128]{2,0,1:T(8,128)(2,1)S(1)} %copy.13), channel_id=1, source_target_pairs={{0,8},{4,12},{8,16},{12,20},{16,24},{20,28},{1,9},{5,13},{9,17},{1... | collective-permute-start | bytes 393224 | tf_op jit(solution)/shard_map/ppermute | solution.py:13
  202.9 10.8 %collective-permute-start.8 = (bf16[256,2,128]{2,0,1:T(8,128)(2,1)S(1)}, bf16[256,2,128]{2,0,1:T(8,128)(2,1)S(1)}, u32[]{:S(2)}, u32[]{:S(2)}) collective-permute-start(bf16[256,2,128]{2,0,1:T(8,128)(2,1)S(1)} %copy.13), channel_id=1, source_target_pairs={{0,12},{4,16},{8,20},{12,24},{16,28},{1,13},{5,17},{9,21},{13,25},... | collective-permute-start | bytes 393224 | tf_op jit(solution)/shard_map/ppermute | solution.py:13
Sparse Core Ops, SparseCore 0:
  8.9 66.1 all-gather.5
  77.0 30.8 all-gather.7
  109.7 36.1 all-gather.9
  147.6 32.1 all-gather.11
  181.6 40.0 all-gather.13
where the time goes:
time: 244 us; the launch traced here: 243 us
  waiting for transfers between devices  152 us (62%)
  starting transfers between devices  33.4 us (14%)
  matrix products  17.8 us (7%)
  blocking collectives  15.7 us (6%)
  between operations  13.5 us (6%)
  other arithmetic  6.45 us (3%)
  local copies, waits for them, and re-layouts  4.87 us (2%)
    all_gather x1, waiting for transfers between devices, on_device(): gathered = lax.all_gather(patches, 'tensor', axis=1, tiled=True)  58.7 us
    ppermute x12, starting transfers between devices, shifted(): return lax.ppermute(x, axis, pairs)  33.3 us
    all_gather x1, waiting for transfers between devices, on_device(): lax.all_gather(w_value, 'seq', axis=0, tiled=True)  32.7 us
    all_gather x1, waiting for transfers between devices, on_device(): lax.all_gather(w_key, 'seq', axis=0, tiled=True)  30.7 us
    all_gather x1, waiting for transfers between devices, on_device(): lax.all_gather(w_query, 'seq', axis=0, tiled=True)  21.1 us
    all_gather x1, blocking collectives, on_device(): lax.all_gather(heads_out, 'tensor', axis=1, tiled=True)  15.7 us
    dot_general x3, matrix products, on_device(): jnp.dot(gathered, piece, preferred_element_type=jnp.float32)  10.6 us
    ppermute x12, waiting for transfers between devices, shifted(): return lax.ppermute(x, axis, pairs)  5.16 us
  transfers between devices with their start and end apart: 17, of which 5 were waited for; matrix products, arithmetic and copies ran while one was open for 10% of the time, Pallas kernels for 0%

commit v1 on v0

--- a/solution.py
+++ b/solution.py
@@ -5,6 +5,16 @@
 
 HS = 128
 SPAN = 3
+
+
+def turned_line(shard, mesh_axis, dim):
+    peers = lax.axis_size(mesh_axis)
+    current, tiles = (shard, [shard])
+    for _ in range(peers - 1):
+        current = lax.ppermute(current, mesh_axis, [(i, (i + 1) % peers) for i in range(peers)])
+        tiles.insert(0, current)
+    row_of_blocks = jnp.concatenate(tiles, axis=dim)
+    return jnp.roll(row_of_blocks, (lax.axis_index(mesh_axis) + 1) * shard.shape[dim], axis=dim)
 
 
 def shifted(x, axis, by):
@@ -19,7 +29,7 @@
     local_heads = col_width // HS
     seq_count = lax.axis_size("seq")
     device = lax.axis_index("seq")
-    gathered = lax.all_gather(patches, "tensor", axis=1, tiled=True)
+    gathered = turned_line(patches, "tensor", 1)
     pieces = (
         lax.all_gather(w_query, "seq", axis=0, tiled=True),
         lax.all_gather(w_key, "seq", axis=0, tiled=True),

time: 244 us -> 178 us (0.73)
  waiting for transfers between devices: 152 us -> 79.8 us
  matrix products: 17.8 us -> 21.9 us
  local copies, waits for them, and re-layouts: 4.87 us -> 8.31 us
    all_gather x1 -> x0, waiting for transfers between devices: 58.7 us -> none  [on_device(): gathered = lax.all_gather(patches, 'tensor', axis=1, tiled=True)]
    ppermute x0 -> x3, waiting for transfers between devices: none -> 53.4 us  [turned_line(): lax.ppermute(current, mesh_axis, [(i, (i + 1) % peers) for i in range(pee...]
    all_gather x1, waiting for transfers between devices: 30.7 us -> 0.01 us  [on_device(): lax.all_gather(w_key, 'seq', axis=0, tiled=True)]
    all_gather x1, waiting for transfers between devices: 21.1 us -> 0.02 us  [on_device(): lax.all_gather(w_query, 'seq', axis=0, tiled=True)]
    all_gather x1, waiting for transfers between devices: 32.7 us -> 14.8 us  [on_device(): lax.all_gather(w_value, 'seq', axis=0, tiled=True)]
    ppermute x12, starting transfers between devices: 33.3 us -> 27.7 us  [shifted(): return lax.ppermute(x, axis, pairs)]
    ppermute x12, waiting for transfers between devices: 5.16 us -> 9.53 us  [shifted(): return lax.ppermute(x, axis, pairs)]
    dot_general x3, matrix products: 10.6 us -> 14.7 us  [on_device(): jnp.dot(gathered, piece, preferred_element_type=jnp.float32)]
  transfers between devices with their start and end apart: 17 -> 19, of which waited for: 5 -> 6; matrix products, arithmetic and copies ran while one was open for 10% -> 19% of each run, Pallas kernels for 0% -> 0%
where the time goes in v1:
time: 178 us; the launch traced here: 177 us
  waiting for transfers between devices  79.8 us (45%)
  starting transfers between devices  31 us (17%)
  matrix products  21.9 us (12%)
  blocking collectives  16 us (9%)
  between operations  13.5 us (8%)
  local copies, waits for them, and re-layouts  8.31 us (5%)
  other arithmetic  6.47 us (4%)
    ppermute x3, waiting for transfers between devices, turned_line(): lax.ppermute(current, mesh_axis, [(i, (i + 1) % peers) for i in range(pee...  53.4 us
    ppermute x12, starting transfers between devices, shifted(): return lax.ppermute(x, axis, pairs)  27.7 us
    all_gather x1, blocking collectives, on_device(): lax.all_gather(heads_out, 'tensor', axis=1, tiled=True)  16 us
    all_gather x1, waiting for transfers between devices, on_device(): lax.all_gather(w_value, 'seq', axis=0, tiled=True)  14.8 us
    dot_general x3, matrix products, on_device(): jnp.dot(gathered, piece, preferred_element_type=jnp.float32)  14.7 us
    ppermute x12, waiting for transfers between devices, shifted(): return lax.ppermute(x, axis, pairs)  9.53 us
    unnamed x23, local copies, waits for them, and re-layouts  7.16 us
    unnamed x7, other arithmetic  4.61 us
  transfers between devices with their start and end apart: 19, of which 6 were waited for; matrix products, arithmetic and copies ran while one was open for 19% of the time, Pallas kernels for 0%

profile of v1, /device:TPU:0, one launch (start us, length us, event | category | flops | bytes accessed | tf_op | source)
XLA Modules:
  0.0 177.0 jit_solution(5426305804534415237)
XLA Ops:
  8.8 3.1 %collective-permute-start = (bf16[256,1536]{1,0:T(8,128)(2,1)}, bf16[256,1536]{1,0:T(8,128)(2,1)S(1)}, u32[]{:S(2)}, u32[]{:S(2)}) collective-permute-start(bf16[256,1536]{1,0:T(8,128)(2,1)} %param.6), channel_id=1, source_target_pairs={{0,1},{1,2},{2,3},{3,0},{4,5},{5,6},{6,7},{7,4},{8,9},{9,10},{10,1... | collective-permute-start | bytes 2359304 | tf_op jit(solution)/shard_map/ppermute | solution.py:14
  11.9 19.8 %collective-permute-done = bf16[256,1536]{1,0:T(8,128)(2,1)S(1)} collective-permute-done((bf16[256,1536]{1,0:T(8,128)(2,1)}, bf16[256,1536]{1,0:T(8,128)(2,1)S(1)}, u32[]{:S(2)}, u32[]{:S(2)}) %collective-permute-start) | collective-permute-done | bytes 786464 | tf_op jit(solution)/shard_map/ppermute | solution.py:14
  34.8 17.3 %collective-permute-done.1 = bf16[256,1536]{1,0:T(8,128)(2,1)S(1)} collective-permute-done((bf16[256,1536]{1,0:T(8,128)(2,1)S(1)}, bf16[256,1536]{1,0:T(8,128)(2,1)S(1)}, u32[]{:S(2)}, u32[]{:S(2)}) %collective-permute-start.1) | collective-permute-done | bytes 786464 | tf_op jit(solution)/shard_map/ppermute | solution.py:14
  54.5 1.1 broadcast_compare_fusion
  55.6 16.2 %collective-permute-done.2 = bf16[256,1536]{1,0:T(8,128)(2,1)S(1)} collective-permute-done((bf16[256,1536]{1,0:T(8,128)(2,1)S(1)}, bf16[256,1536]{1,0:T(8,128)(2,1)S(1)}, u32[]{:S(2)}, u32[]{:S(2)}) %collective-permute-start.2) | collective-permute-done | bytes 786464 | tf_op jit(solution)/shard_map/ppermute | solution.py:14
  72.8 1.0 constant_dynamic-update-slice_fusion.6
  74.8 1.0 constant_dynamic-update-slice_fusion.4
  76.7 1.0 constant_dynamic-update-slice_fusion.2
  77.7 1.1 constant_dynamic-update-slice_fusion.1
  78.8 1.0 constant_dynamic-update-slice_fusion
  79.8 4.9 %fusion.15 = bf16[256,256]{0,1:T(8,128)(2,1)S(1)} fusion(bf16[6144,256]{1,0:T(8,128)(2,1)} %all-gather.9.cloned.1.call-done, bf16[256,12288]{1,0:T(8,128)(2,1)} %constant_dynamic-update-slice_fusion, s32[]{:T(128)S(6)} %select_n.86), kind=kOutput, calls=%fused_computation.15 | convolution fusion | flops 805371904 | bytes 6422532 | tf_op jit(solution)/shard_map/dot_general | solution.py:38
  84.8 1.3 collective-permute-start.9
  86.1 3.6 %collective-permute-start.10 = (bf16[256,2,128]{2,0,1:T(8,128)(2,1)S(1)}, bf16[256,2,128]{2,0,1:T(8,128)(2,1)S(1)}, u32[]{:S(2)}, u32[]{:S(2)}) collective-permute-start(bf16[256,2,128]{2,0,1:T(8,128)(2,1)S(1)} %copy.13), channel_id=1, source_target_pairs={{0,8},{4,12},{8,16},{12,20},{16,24},{20,28},{1,9},{5,13},{9,17},{1... | collective-permute-start | bytes 393224 | tf_op jit(solution)/shard_map/ppermute | solution.py:23
  89.7 4.3 %collective-permute-start.11 = (bf16[256,2,128]{2,0,1:T(8,128)(2,1)S(1)}, bf16[256,2,128]{2,0,1:T(8,128)(2,1)S(1)}, u32[]{:S(2)}, u32[]{:S(2)}) collective-permute-start(bf16[256,2,128]{2,0,1:T(8,128)(2,1)S(1)} %copy.13), channel_id=1, source_target_pairs={{0,12},{4,16},{8,20},{12,24},{16,28},{1,13},{5,17},{9,21},{13,25},... | collective-permute-start | bytes 393224 | tf_op jit(solution)/shard_map/ppermute | solution.py:23
  94.1 1.3 collective-permute-start.12
  95.4 1.3 collective-permute-start.13
  96.7 4.9 %fusion.12 = bf16[256,256]{0,1:T(8,128)(2,1)S(1)} fusion(bf16[6144,256]{1,0:T(8,128)(2,1)} %all-gather.7.cloned.1.call-done, bf16[256,12288]{1,0:T(8,128)(2,1)} %constant_dynamic-update-slice_fusion, s32[]{:T(128)S(6)} %select_n.86), kind=kOutput, calls=%fused_computation.14 | convolution fusion | flops 805371904 | bytes 6422532 | tf_op jit(solution)/shard_map/dot_general | solution.py:38
  101.6 14.8 %all-gather.5.cloned.1.call-done = bf16[6144,256]{1,0:T(8,128)(2,1)} async-done(((bf16[768,256]{1,0:T(8,128)(2,1)}), bf16[6144,256]{1,0:T(8,128)(2,1)}) %all-gather.5.cloned.1.call-update) | async-done | bytes 3145744 | tf_op jit(solution)/shard_map/all_gather | solution.py:36
  116.5 4.9 %fusion.9 = bf16[256,256]{0,1:T(8,128)(2,1)S(1)} fusion(bf16[6144,256]{1,0:T(8,128)(2,1)} %all-gather.5.cloned.1.call-done, bf16[256,12288]{1,0:T(8,128)(2,1)} %constant_dynamic-update-slice_fusion, s32[]{:T(128)S(6)} %select_n.86), kind=kOutput, calls=%fused_computation.13 | convolution fusion | flops 805371904 | bytes 6422532 | tf_op jit(solution)/shard_map/dot_general | solution.py:38
  121.4 1.3 collective-permute-start.14
  122.7 2.2 %collective-permute-start.3 = (bf16[256,2,128]{0,2,1:T(8,128)(2,1)S(1)}, bf16[256,2,128]{0,2,1:T(8,128)(2,1)S(1)}, u32[]{:S(2)}, u32[]{:S(2)}) collective-permute-start(bf16[256,2,128]{0,2,1:T(8,128)(2,1)S(1)} %bitcast.17), channel_id=1, source_target_pairs={{0,4},{4,8},{8,12},{12,16},{16,20},{20,24},{24,28},{1,5},{5,9},{9,... | collective-permute-start | bytes 393224 | tf_op jit(solution)/shard_map/ppermute | solution.py:23
  124.9 4.4 %collective-permute-start.4 = (bf16[256,2,128]{0,2,1:T(8,128)(2,1)S(1)}, bf16[256,2,128]{0,2,1:T(8,128)(2,1)S(1)}, u32[]{:S(2)}, u32[]{:S(2)}) collective-permute-start(bf16[256,2,128]{0,2,1:T(8,128)(2,1)S(1)} %bitcast.18), channel_id=1, source_target_pairs={{0,8},{4,12},{8,16},{12,20},{16,24},{20,28},{1,9},{5,13},{9,17},{1... | collective-permute-start | bytes 393224 | tf_op jit(solution)/shard_map/ppermute | solution.py:23
  129.4 4.0 %collective-permute-start.5 = (bf16[256,2,128]{0,2,1:T(8,128)(2,1)S(1)}, bf16[256,2,128]{0,2,1:T(8,128)(2,1)S(1)}, u32[]{:S(2)}, u32[]{:S(2)}) collective-permute-start(bf16[256,2,128]{0,2,1:T(8,128)(2,1)S(1)} %bitcast.19), channel_id=1, source_target_pairs={{0,12},{4,16},{8,20},{12,24},{16,28},{1,13},{5,17},{9,21},{13,25},... | collective-permute-start | bytes 393224 | tf_op jit(solution)/shard_map/ppermute | solution.py:23
  133.5 1.3 collective-permute-start.6
  134.8 1.3 collective-permute-start.7
  136.1 1.5 collective-permute-start.8
  137.7 5.2 %collective-permute-done.7 = bf16[256,2,128]{0,2,1:T(8,128)(2,1)S(1)} collective-permute-done((bf16[256,2,128]{0,2,1:T(8,128)(2,1)S(1)}, bf16[256,2,128]{0,2,1:T(8,128)(2,1)S(1)}, u32[]{:S(2)}, u32[]{:S(2)}) %collective-permute-start.7) | collective-permute-done | bytes 131104 | tf_op jit(solution)/shard_map/ppermute | solution.py:23
  142.9 4.3 %collective-permute-done.8 = bf16[256,2,128]{0,2,1:T(8,128)(2,1)S(1)} collective-permute-done((bf16[256,2,128]{0,2,1:T(8,128)(2,1)S(1)}, bf16[256,2,128]{0,2,1:T(8,128)(2,1)S(1)}, u32[]{:S(2)}, u32[]{:S(2)}) %collective-permute-start.8) | collective-permute-done | bytes 131104 | tf_op jit(solution)/shard_map/ppermute | solution.py:23
  147.3 1.5 exponential_reduce_fusion
  148.8 1.9 %fusion.18 = bf16[2,128,256]{2,1,0:T(8,128)(2,1)S(1)} fusion(bf16[1792,2,128]{0,2,1:T(8,128)(2,1)S(1)} %constant_dynamic-update-slice_fusion.8, f32[2,256]{1,0:T(2,128)S(1)} %exponential_reduce_fusion, bf16[256,2,128]{0,2,1:T(8,128)(2,1)S(1)} %bitcast.25, bf16[1792,2,128]{2,0,1:T(8,128)(2,1)S(1)} %constant_dynamic-update-slice_fusion.16, ...), kind=kOutput, calls=%fused_computation.16 | convolution fusion | flops 474417408 | bytes 2557952 | tf_op jit(solution)/shard_map/hqk,khd->qhd/dot_general | solution.py:66
  150.7 16.0 %all_gather.18 = bf16[256,1024]{0,1:T(8,128)(2,1)S(1)} all-gather(bf16[256,256]{0,1:T(8,128)(2,1)S(1)} %bitcast.26), channel_id=1, replica_groups=mesh['seq'=8,'tensor'=4] {'tensor'}, dimensions={1}, use_global_device_ids=true | all-gather | bytes 655360 | tf_op jit(solution)/shard_map/all_gather | solution.py:72
  166.7 3.8 %convolution_convert_fusion = bf16[256,1536]{1,0:T(8,128)(2,1)} fusion(bf16[256,1024]{0,1:T(8,128)(2,1)S(1)} %all_gather.18, bf16[1024,1536]{1,0:T(8,128)(2,1)} %all-gather.11.cloned.1.call-done), kind=kOutput, calls=%fused_computation.5 | convolution fusion | flops 805699584 | bytes 4456448 | tf_op jit(solution)/shard_map/dot_general | solution.py:71
  (53 shorter events, 10.9 us)
Async XLA Ops:
  6.5 68.2 %copy-start = (bf16[256,1536]{1,0:T(8,128)(2,1)S(1)}, bf16[256,1536]{1,0:T(8,128)(2,1)}, u32[]{:S(2)}) copy-start(bf16[256,1536]{1,0:T(8,128)(2,1)} %param.6) | copy-start | bytes 2359300
  6.5 73.3 %all-gather.9.cloned.1.call-start = ((), (), s32[]{:S(2)}) async-start(), calls=%async_computation.2 | async-start | bytes 3538944 | tf_op jit(solution)/shard_map/all_gather | solution.py:35
  7.3 89.4 %all-gather.7.cloned.1.call-start = ((), (), s32[]{:S(2)}) async-start(), calls=%async_computation.1 | async-start | bytes 3538944 | tf_op jit(solution)/shard_map/all_gather | solution.py:34
  8.0 108.4 %all-gather.5.cloned.1.call-start = ((), (), s32[]{:S(2)}) async-start(), calls=%async_computation | async-start | bytes 3538944 | tf_op jit(solution)/shard_map/all_gather | solution.py:36
  8.7 157.9 %all-gather.11.cloned.1.call-start = ((), (), s32[]{:S(2)}) async-start(), calls=%async_computation.3 | async-start | bytes 3538944 | tf_op jit(solution)/shard_map/all_gather | solution.py:70
  8.8 22.9 %collective-permute-start = (bf16[256,1536]{1,0:T(8,128)(2,1)}, bf16[256,1536]{1,0:T(8,128)(2,1)S(1)}, u32[]{:S(2)}, u32[]{:S(2)}) collective-permute-start(bf16[256,1536]{1,0:T(8,128)(2,1)} %param.6), channel_id=1, source_target_pairs={{0,1},{1,2},{2,3},{3,0},{4,5},{5,6},{6,7},{7,4},{8,9},{9,10},{10,1... | collective-permute-start | bytes 2359304 | tf_op jit(solution)/shard_map/ppermute | solution.py:14
  31.7 20.5 %collective-permute-start.1 = (bf16[256,1536]{1,0:T(8,128)(2,1)S(1)}, bf16[256,1536]{1,0:T(8,128)(2,1)S(1)}, u32[]{:S(2)}, u32[]{:S(2)}) collective-permute-start(bf16[256,1536]{1,0:T(8,128)(2,1)S(1)} %collective-permute-done), channel_id=1, source_target_pairs={{0,1},{1,2},{2,3},{3,0},{4,5},{5,6},{6,7},{7,4},{8,9},{9,10},{10,1... | collective-permute-start | bytes 2359304 | tf_op jit(solution)/shard_map/ppermute | solution.py:14
  52.2 19.6 %collective-permute-start.2 = (bf16[256,1536]{1,0:T(8,128)(2,1)S(1)}, bf16[256,1536]{1,0:T(8,128)(2,1)S(1)}, u32[]{:S(2)}, u32[]{:S(2)}) collective-permute-start(bf16[256,1536]{1,0:T(8,128)(2,1)S(1)} %collective-permute-done.1), channel_id=1, source_target_pairs={{0,1},{1,2},{2,3},{3,0},{4,5},{5,6},{6,7},{7,4},{8,9},{9,10},{10,1... | collective-permute-start | bytes 2359304 | tf_op jit(solution)/shard_map/ppermute | solution.py:14
  84.8 36.5 %collective-permute-start.9 = (bf16[256,2,128]{2,0,1:T(8,128)(2,1)S(1)}, bf16[256,2,128]{2,0,1:T(8,128)(2,1)S(1)}, u32[]{:S(2)}, u32[]{:S(2)}) collective-permute-start(bf16[256,2,128]{2,0,1:T(8,128)(2,1)S(1)} %copy.13), channel_id=1, source_target_pairs={{0,4},{4,8},{8,12},{12,16},{16,20},{20,24},{24,28},{1,5},{5,9},{9,... | collective-permute-start | bytes 393224 | tf_op jit(solution)/shard_map/ppermute | solution.py:23
  86.1 36.6 %collective-permute-start.10 = (bf16[256,2,128]{2,0,1:T(8,128)(2,1)S(1)}, bf16[256,2,128]{2,0,1:T(8,128)(2,1)S(1)}, u32[]{:S(2)}, u32[]{:S(2)}) collective-permute-start(bf16[256,2,128]{2,0,1:T(8,128)(2,1)S(1)} %copy.13), channel_id=1, source_target_pairs={{0,8},{4,12},{8,16},{12,20},{16,24},{20,28},{1,9},{5,13},{9,17},{1... | collective-permute-start | bytes 393224 | tf_op jit(solution)/shard_map/ppermute | solution.py:23
  89.7 35.2 %collective-permute-start.11 = (bf16[256,2,128]{2,0,1:T(8,128)(2,1)S(1)}, bf16[256,2,128]{2,0,1:T(8,128)(2,1)S(1)}, u32[]{:S(2)}, u32[]{:S(2)}) collective-permute-start(bf16[256,2,128]{2,0,1:T(8,128)(2,1)S(1)} %copy.13), channel_id=1, source_target_pairs={{0,12},{4,16},{8,20},{12,24},{16,28},{1,13},{5,17},{9,21},{13,25},... | collective-permute-start | bytes 393224 | tf_op jit(solution)/shard_map/ppermute | solution.py:23
  94.1 35.3 %collective-permute-start.12 = (bf16[256,2,128]{2,0,1:T(8,128)(2,1)S(1)}, bf16[256,2,128]{2,0,1:T(8,128)(2,1)S(1)}, u32[]{:S(2)}, u32[]{:S(2)}) collective-permute-start(bf16[256,2,128]{2,0,1:T(8,128)(2,1)S(1)} %copy.13), channel_id=1, source_target_pairs={{4,0},{8,4},{12,8},{16,12},{20,16},{24,20},{28,24},{5,1},{9,5},{13... | collective-permute-start | bytes 393224 | tf_op jit(solution)/shard_map/ppermute | solution.py:23
  95.4 38.1 %collective-permute-start.13 = (bf16[256,2,128]{2,0,1:T(8,128)(2,1)S(1)}, bf16[256,2,128]{2,0,1:T(8,128)(2,1)S(1)}, u32[]{:S(2)}, u32[]{:S(2)}) collective-permute-start(bf16[256,2,128]{2,0,1:T(8,128)(2,1)S(1)} %copy.13), channel_id=1, source_target_pairs={{8,0},{12,4},{16,8},{20,12},{24,16},{28,20},{9,1},{13,5},{17,9},{2... | collective-permute-start | bytes 393224 | tf_op jit(solution)/shard_map/ppermute | solution.py:23
  101.6 45.6 %copy-start.1 = (pred[256,1792]{1,0:T(8,128)(4,1)S(1)}, pred[256,1792]{1,0:T(8,128)(4,1)}, u32[]{:S(2)}) copy-start(pred[256,1792]{1,0:T(8,128)(4,1)} %broadcast_compare_fusion) | copy-start | bytes 1376260
  121.4 13.4 %collective-permute-start.14 = (bf16[256,2,128]{2,0,1:T(8,128)(2,1)S(1)}, bf16[256,2,128]{2,0,1:T(8,128)(2,1)S(1)}, u32[]{:S(2)}, u32[]{:S(2)}) collective-permute-start(bf16[256,2,128]{2,0,1:T(8,128)(2,1)S(1)} %copy.13), channel_id=1, source_target_pairs={{12,0},{16,4},{20,8},{24,12},{28,16},{13,1},{17,5},{21,9},{25,13},... | collective-permute-start | bytes 393224 | tf_op jit(solution)/shard_map/ppermute | solution.py:23
  122.7 13.4 %collective-permute-start.3 = (bf16[256,2,128]{0,2,1:T(8,128)(2,1)S(1)}, bf16[256,2,128]{0,2,1:T(8,128)(2,1)S(1)}, u32[]{:S(2)}, u32[]{:S(2)}) collective-permute-start(bf16[256,2,128]{0,2,1:T(8,128)(2,1)S(1)} %bitcast.17), channel_id=1, source_target_pairs={{0,4},{4,8},{8,12},{12,16},{16,20},{20,24},{24,28},{1,5},{5,9},{9,... | collective-permute-start | bytes 393224 | tf_op jit(solution)/shard_map/ppermute | solution.py:23
  124.9 12.7 %collective-permute-start.4 = (bf16[256,2,128]{0,2,1:T(8,128)(2,1)S(1)}, bf16[256,2,128]{0,2,1:T(8,128)(2,1)S(1)}, u32[]{:S(2)}, u32[]{:S(2)}) collective-permute-start(bf16[256,2,128]{0,2,1:T(8,128)(2,1)S(1)} %bitcast.18), channel_id=1, source_target_pairs={{0,8},{4,12},{8,16},{12,20},{16,24},{20,28},{1,9},{5,13},{9,17},{1... | collective-permute-start | bytes 393224 | tf_op jit(solution)/shard_map/ppermute | solution.py:23
  129.4 8.3 %collective-permute-start.5 = (bf16[256,2,128]{0,2,1:T(8,128)(2,1)S(1)}, bf16[256,2,128]{0,2,1:T(8,128)(2,1)S(1)}, u32[]{:S(2)}, u32[]{:S(2)}) collective-permute-start(bf16[256,2,128]{0,2,1:T(8,128)(2,1)S(1)} %bitcast.19), channel_id=1, source_target_pairs={{0,12},{4,16},{8,20},{12,24},{16,28},{1,13},{5,17},{9,21},{13,25},... | collective-permute-start | bytes 393224 | tf_op jit(solution)/shard_map/ppermute | solution.py:23
  133.5 4.2 %collective-permute-start.6 = (bf16[256,2,128]{0,2,1:T(8,128)(2,1)S(1)}, bf16[256,2,128]{0,2,1:T(8,128)(2,1)S(1)}, u32[]{:S(2)}, u32[]{:S(2)}) collective-permute-start(bf16[256,2,128]{0,2,1:T(8,128)(2,1)S(1)} %bitcast.20), channel_id=1, source_target_pairs={{4,0},{8,4},{12,8},{16,12},{20,16},{24,20},{28,24},{5,1},{9,5},{13... | collective-permute-start | bytes 393224 | tf_op jit(solution)/shard_map/ppermute | solution.py:23
  134.8 8.1 %collective-permute-start.7 = (bf16[256,2,128]{0,2,1:T(8,128)(2,1)S(1)}, bf16[256,2,128]{0,2,1:T(8,128)(2,1)S(1)}, u32[]{:S(2)}, u32[]{:S(2)}) collective-permute-start(bf16[256,2,128]{0,2,1:T(8,128)(2,1)S(1)} %bitcast.21), channel_id=1, source_target_pairs={{8,0},{12,4},{16,8},{20,12},{24,16},{28,20},{9,1},{13,5},{17,9},{2... | collective-permute-start | bytes 393224 | tf_op jit(solution)/shard_map/ppermute | solution.py:23
  136.1 11.1 %collective-permute-start.8 = (bf16[256,2,128]{0,2,1:T(8,128)(2,1)S(1)}, bf16[256,2,128]{0,2,1:T(8,128)(2,1)S(1)}, u32[]{:S(2)}, u32[]{:S(2)}) collective-permute-start(bf16[256,2,128]{0,2,1:T(8,128)(2,1)S(1)} %bitcast.22), channel_id=1, source_target_pairs={{12,0},{16,4},{20,8},{24,12},{28,16},{13,1},{17,5},{21,9},{25,13},... | collective-permute-start | bytes 393224 | tf_op jit(solution)/shard_map/ppermute | solution.py:23
Sparse Core Ops, SparseCore 0:
  9.2 34.8 all-gather.8
  46.0 32.2 all-gather.6
  80.2 36.1 all-gather.4
  118.2 36.2 all-gather.10
